TPU v7x, 32 devices: a whole 2x2x4 slice. The times are simulated.
32 devices in a mesh: dp: 2 (over y), expert: 16 (over z, x, core).
Axes of the slice: x: 2, y: 2, z: 4, core: 2. Of those that a mesh axis runs over, the one named last changes fastest.
Arguments:
- tokens: bfloat16 [4096, 2048], P(('dp', 'expert')), may hold values from -6 to 6
- grad_out: bfloat16 [4096, 2048], P(('dp', 'expert')), may hold values from -6 to 6
- expert_ids: int32 [4096, 8], P(('dp', 'expert')), may hold values from 0 to 15, all different within a row; in each aligned block of 128 rows (0 to 127, 128 to 255, ...) at most 72 rows name the same one
- route_weight: bfloat16 [4096, 8], P(('dp', 'expert')), may hold values from 0.049804688 to 1
- w_gate: bfloat16 [16, 2048, 384], P('expert', 'dp'), may hold values from -0.125 to 0.125
- w_up: bfloat16 [16, 2048, 384], P('expert', 'dp'), may hold values from -0.125 to 0.125
- w_down: bfloat16 [16, 384, 2048], P('expert', None, 'dp'), may hold values from -0.3125 to 0.3125
Outputs:
- grad_tokens: bfloat16 [4096, 2048], P(('dp', 'expert'))
- grad_route: bfloat16 [4096, 8], P(('dp', 'expert'))
Inputs may be any that keep to these rules, and one draw needn't show every extreme that they name: `expert_ids`: each row names 8 different experts; among the 128 rows of one device no expert is named by more than 72 rows, and in every draw some expert is named by exactly 72 rows of some device.
All inputs are finite; a program needn't handle non-finite values.
Results may differ from a plain program's by a relative error of at most 0.012.
Values may be sent and summed in bfloat16 or wider, within the bound.
A program may use at most 128 MiB of HBM per device.

v0:
```python
import jax
import jax.numpy as jnp
from jax import lax
from jax.sharding import PartitionSpec as P


def expert_rows(x_rows, g_rows, weight_rows, gate_mat, up_mat, down_mat):
    gate_pre = jnp.dot(x_rows, gate_mat, preferred_element_type=jnp.float32)
    up_pre = jnp.dot(x_rows, up_mat, preferred_element_type=jnp.float32)
    sigmoid_gate = jax.nn.sigmoid(gate_pre)
    active = gate_pre * sigmoid_gate
    hidden = active * up_pre
    back_hidden = jnp.dot(g_rows, down_mat.T, preferred_element_type=jnp.float32)
    route_grad = jnp.sum(hidden * back_hidden, axis=1)
    scaled = weight_rows.astype(jnp.float32)[:, None] * back_hidden
    slope = sigmoid_gate * (1.0 + gate_pre * (1.0 - sigmoid_gate))
    d_gate = (scaled * up_pre * slope).astype(jnp.bfloat16)
    d_up = (scaled * active).astype(jnp.bfloat16)
    input_grad = jnp.dot(d_gate, gate_mat.T, preferred_element_type=jnp.float32) + jnp.dot(
        d_up, up_mat.T, preferred_element_type=jnp.float32
    )
    return (input_grad.astype(jnp.bfloat16), route_grad.astype(jnp.bfloat16))


def fetch_rows(tokens, grad_out, flat_weight, assign_of, top_k):
    token_of = assign_of // top_k
    rows_x = jnp.take(tokens, token_of, axis=0, mode="fill", fill_value=0)
    rows_g = jnp.take(grad_out, token_of, axis=0, mode="fill", fill_value=0)
    rows_w = jnp.take(flat_weight, assign_of, axis=0, mode="fill", fill_value=0)
    return (rows_x, rows_g, rows_w)


def per_device(tokens, grad_out, expert_ids, route_weight, w_gate, w_up, w_down):
    tok_rows, width_model = tokens.shape
    top_k = expert_ids.shape[1]
    n_assign = tok_rows * top_k
    n_expert = lax.axis_size("expert")
    capacity = 9 * tok_rows * top_k // (8 * n_expert)
    slots_all = n_expert * capacity
    gate_mat, up_mat, down_mat = (
        lax.all_gather(w_gate[0], "dp", axis=0, tiled=True),
        lax.all_gather(w_up[0], "dp", axis=0, tiled=True),
        lax.all_gather(w_down[0], "dp", axis=1, tiled=True),
    )
    flat_ids = expert_ids.reshape(-1)
    flat_weight = route_weight.reshape(-1)
    onehot = (flat_ids[:, None] == jnp.arange(n_expert, dtype=jnp.int32)[None, :]).astype(jnp.int32)
    earlier = jnp.cumsum(onehot, axis=0) - onehot
    slot_of = jnp.sum(earlier * onehot, axis=1)
    placed = flat_ids * capacity + slot_of
    assign_index = jnp.arange(n_assign, dtype=jnp.int32)
    slot_assign = (
        jnp.full((slots_all,), n_assign, jnp.int32).at[placed].set(assign_index, mode="drop")
    )
    send_x, send_g, send_w = fetch_rows(tokens, grad_out, flat_weight, slot_assign, top_k)
    send_x = send_x.reshape(n_expert, capacity, width_model)
    send_g = send_g.reshape(n_expert, capacity, width_model)
    send_w = send_w.reshape(n_expert, capacity)
    got_x, got_g, got_w = (
        lax.all_to_all(send_x, "expert", split_axis=0, concat_axis=0, tiled=True),
        lax.all_to_all(send_g, "expert", split_axis=0, concat_axis=0, tiled=True),
        lax.all_to_all(send_w, "expert", split_axis=0, concat_axis=0, tiled=True),
    )
    out_grad, out_route = expert_rows(
        got_x.reshape(slots_all, width_model),
        got_g.reshape(slots_all, width_model),
        got_w.reshape(slots_all),
        gate_mat,
        up_mat,
        down_mat,
    )
    out_grad = out_grad.reshape(n_expert, capacity, width_model)
    out_route = out_route.reshape(n_expert, capacity)
    back_grad, back_route = (
        lax.all_to_all(out_grad, "expert", split_axis=0, concat_axis=0, tiled=True),
        lax.all_to_all(out_route, "expert", split_axis=0, concat_axis=0, tiled=True),
    )
    part_flat = back_grad.reshape(slots_all, width_model)[placed]
    route_flat = back_route.reshape(slots_all)[placed]
    part_rows = part_flat.reshape(tok_rows, top_k, width_model)
    grad_tokens = jnp.sum(part_rows.astype(jnp.float32), axis=1).astype(jnp.bfloat16)
    grad_route = route_flat.reshape(tok_rows, top_k)
    return (grad_tokens, grad_route)


def solution(mesh):
    return jax.shard_map(
        per_device,
        mesh=mesh,
        in_specs=(
            P(("dp", "expert"), None),
            P(("dp", "expert"), None),
            P(("dp", "expert"), None),
            P(("dp", "expert"), None),
            P("expert", "dp", None),
            P("expert", "dp", None),
            P("expert", None, "dp"),
        ),
        out_specs=(P(("dp", "expert"), None), P(("dp", "expert"), None)),
        check_vma=False,
    )
```

profile of v0, /device:TPU:11, one launch (start us, length us, event | category | flops | bytes accessed | tf_op | source)
XLA Modules:
  0.0 429.3 jit_solution(9125871058928897859)
XLA Ops:
  7.2 0.7 broadcast_multiply_fusion
  7.9 0.8 copy.19
  8.9 0.8 copy.23
  10.0 4.5 %reduce-window.6 = s32[16,8,128]{2,1,0:T(8,128)S(1)} reduce-window(s32[16,8,128]{2,1,0:T(8,128)S(1)} %fusion.18, s32[]{:T(128)} %constant.47.clone.1), window={size=1x1x128 pad=0_0x0_0x127_0}, to_apply=%region_0.0 | reduce-window | flops 2080768 | bytes 131076 | tf_op jit(solution)/shard_map/reduce-window
  15.0 4.3 %scatter_custom_fusion = s32[1152]{0:T(1024)S(1)} fusion(s32[1024]{0:T(1024)S(1)} %bitcast.55, s32[1024]{0:T(1024)S(1)} %iota.11, s32[]{:T(128)} %constant.31.clone.1), kind=kCustom, calls=%fused_computation.51 | custom fusion | bytes 4612 | tf_op jit(solution)/shard_map/scatter | solution.py:53
  19.4 7.3 %gather_fusion = bf16[1152]{0:T(1024)(128)(2,1)S(1)} fusion(bf16[1024]{0:T(1024)(128)(2,1)S(1)} %reshape.140, s32[2048]{0:T(1024)S(1)} %pad_clamp_fusion.1), kind=kCustom, calls=%fused_computation.2 | custom fusion | bytes 9216 | tf_op jit(solution)/shard_map/jit(_take)/gather | solution.py:29
  26.7 0.7 select_n.53
  27.4 6.5 %all-to-all-start = ((bf16[16,1,72]{2,1,0:T(2,128)(2,1)}), bf16[16,1,72]{2,1,0:T(2,128)(2,1)S(1)}, u32[]{:S(2)}, u32[]{:S(2)}) async-start(bf16[16,1,72]{2,1,0:T(2,128)(2,1)} %select_n.53), calls=%async_computation | async-start | bytes 16384 | tf_op jit(solution)/shard_map/all_to_all | solution.py:62
  33.9 5.9 %gather_fusion.4 = bf16[1152,2048]{1,0:T(8,128)(2,1)} fusion(bf16[128,2048]{1,0:T(8,128)(2,1)S(1)} %copy-done, s32[2048]{0:T(1024)S(1)} %pad_clamp_fusion), kind=kCustom, calls=%fused_computation.1.clone | custom fusion | bytes 9441792 | tf_op jit(solution)/shard_map/jit(_take)/gather | solution.py:27
  39.8 5.9 %gather_fusion.3 = bf16[1152,2048]{1,0:T(8,128)(2,1)} fusion(bf16[128,2048]{1,0:T(8,128)(2,1)S(1)} %copy-done.1, s32[2048]{0:T(1024)S(1)} %pad_clamp_fusion), kind=kCustom, calls=%fused_computation.clone | custom fusion | bytes 9441792 | tf_op jit(solution)/shard_map/jit(_take)/gather | solution.py:28
  45.8 8.5 %broadcast_select_fusion.1 = (bf16[1152,2048]{1,0:T(8,128)(2,1)}, bf16[1152,2048]{1,0:T(8,128)(2,1)}) fusion(bf16[1152,2048]{1,0:T(8,128)(2,1)} %gather_fusion.3, pred[1152]{0:T(1024)(128)(4,1)S(1)} %get-tuple-element.7, bf16[1152,2048]{1,0:T(8,128)(2,1)} %gather_fusion.4), kind=kLoop, calls=%fused_computation.9 | loop fusion | flops 4718592 | bytes 18875520 | tf_op jit(solution)/shard_map/jit(_take)/select_n | solution.py:28
  54.3 109.6 %all_to_all.27 = bf16[16,72,2048]{2,1,0:T(8,128)(2,1)} all-to-all(bf16[16,72,2048]{2,1,0:T(8,128)(2,1)} %bitcast.48), channel_id=1, replica_groups=mesh['dp'=2,'expert'=16] {'expert'}, dimensions={0} | all-to-all | bytes 9437184 | tf_op jit(solution)/shard_map/all_to_all | solution.py:60
  163.8 5.3 %all-to-all-start.1 = ((bf16[16,72,2048]{2,1,0:T(8,128)(2,1)}), bf16[16,72,2048]{2,1,0:T(8,128)(2,1)}, u32[]{:S(2)}, u32[]{:S(2)}) async-start(bf16[16,72,2048]{2,1,0:T(8,128)(2,1)} %bitcast.47), calls=%async_computation.1 | async-start | bytes 9437184 | tf_op jit(solution)/shard_map/all_to_all | solution.py:61
  169.1 0.7 all-gather.11.cloned.1.call-update
  169.9 0.7 all-gather.9.cloned.1.call-update
  171.4 27.7 %all-gather.11.cloned.1.call-done = bf16[1,2048,384]{2,1,0:T(8,128)(2,1)} async-done(((bf16[1,1024,384]{2,1,0:T(8,128)(2,1)}), bf16[1,2048,384]{2,1,0:T(8,128)(2,1)}) %all-gather.11.cloned.1.call-update) | async-done | bytes 1572880 | tf_op jit(solution)/shard_map/all_gather | solution.py:41
  199.1 5.1 %fusion.4 = f32[1152,384]{0,1:T(8,128)S(1)} fusion(bf16[1152,2048]{1,0:T(8,128)(2,1)} %bitcast.50, bf16[1,2048,384]{2,1,0:T(8,128)(2,1)} %all-gather.11.cloned.1.call-done), kind=kOutput, calls=%fused_computation.18 | convolution fusion | flops 1811939328 | bytes 8060928 | tf_op jit(solution)/shard_map/dot_general | solution.py:8
  204.2 23.7 %all-gather.9.cloned.1.call-done = bf16[1,2048,384]{2,1,0:T(8,128)(2,1)} async-done(((bf16[1,1024,384]{2,1,0:T(8,128)(2,1)}), bf16[1,2048,384]{2,1,0:T(8,128)(2,1)}) %all-gather.9.cloned.1.call-update) | async-done | bytes 1572880 | tf_op jit(solution)/shard_map/all_gather | solution.py:42
  227.9 6.3 %fusion.7 = f32[1152,384]{0,1:T(8,128)} fusion(bf16[1152,2048]{1,0:T(8,128)(2,1)} %bitcast.51, bf16[1,2048,384]{2,1,0:T(8,128)(2,1)} %all-gather.9.cloned.1.call-done), kind=kOutput, calls=%fused_computation.21 | convolution fusion | flops 1811939328 | bytes 8060928 | tf_op jit(solution)/shard_map/dot_general | solution.py:9
  234.2 22.5 %all-gather.7.cloned.1.call-done = bf16[1,384,2048]{2,1,0:T(8,128)(2,1)} async-done(((bf16[1,384,1024]{2,1,0:T(8,128)(2,1)}), bf16[1,384,2048]{2,1,0:T(8,128)(2,1)}) %all-gather.7.cloned.1.call-update) | async-done | bytes 1572880 | tf_op jit(solution)/shard_map/all_gather | solution.py:43
  256.7 16.1 %all-to-all-done.1 = bf16[16,72,2048]{2,1,0:T(8,128)(2,1)} async-done(((bf16[16,72,2048]{2,1,0:T(8,128)(2,1)}), bf16[16,72,2048]{2,1,0:T(8,128)(2,1)}, u32[]{:S(2)}, u32[]{:S(2)}) %all-to-all-start.1) | async-done | bytes 4718624 | tf_op jit(solution)/shard_map/all_to_all | solution.py:61
  272.8 6.8 %multiply_reduce_fusion = (bf16[1152]{0:T(1024)(128)(2,1)S(1)}, f32[1152,384]{0,1:T(8,128)}) fusion(f32[1152,384]{0,1:T(8,128)} %fusion.7, f32[1152,384]{0,1:T(8,128)S(1)} %fusion.4, bf16[1152,2048]{1,0:T(8,128)(2,1)} %bitcast.5, bf16[1,384,2048]{2,1,0:T(8,128)(2,1)} %all-gather.7.cloned.1.call-done), kind=kOutput, calls=%fused_computation.11 | convolution fusion | flops 1815034752 | bytes 11602176 | tf_op jit(solution)/shard_map/dot_general | solution.py:13
  279.6 0.7 convert_element_type.52
  280.3 4.8 %all-to-all-start.4 = ((bf16[16,1,72]{2,1,0:T(2,128)(2,1)}), bf16[16,1,72]{2,1,0:T(2,128)(2,1)S(1)}, u32[]{:S(2)}, u32[]{:S(2)}) async-start(bf16[16,1,72]{2,1,0:T(2,128)(2,1)} %convert_element_type.52), calls=%async_computation.4 | async-start | bytes 16384 | tf_op jit(solution)/shard_map/all_to_all | solution.py:76
  285.1 5.6 %fusion.2 = f32[1152,2048]{1,0:T(8,128)S(1)} fusion(bf16[1,2048,384]{2,1,0:T(8,128)(2,1)} %all-gather.11.cloned.1.call-done, f32[1152,384]{0,1:T(8,128)S(1)} %fusion.4, f32[1152,384]{0,1:T(8,128)} %fusion.7, f32[1152,384]{0,1:T(8,128)} %get-tuple-element.12, f32[1152]{0:T(1024)S(1)} %reshape.150), kind=kOutput, calls=%fused_computation.16 | convolution fusion | flops 1816805376 | bytes 16323072 | tf_op jit(solution)/shard_map/dot_general | solution.py:19
  290.8 4.5 %fusion = bf16[1152,2048]{1,0:T(8,128)(2,1)} fusion(f32[1152,2048]{1,0:T(8,128)S(1)} %fusion.2, bf16[1,2048,384]{2,1,0:T(8,128)(2,1)S(1)} %copy-done.3, f32[1152,384]{0,1:T(8,128)S(1)} %copy-done.2, f32[1152]{0:T(1024)S(1)} %reshape.150, f32[1152,384]{0,1:T(8,128)S(1)} %fusion.4), kind=kOutput, calls=%fused_computation.7 | convolution fusion | flops 1819754496 | bytes 19272192 | tf_op jit(solution)/shard_map/dot_general | solution.py:19
  295.3 6.0 %all-to-all-start.3 = ((bf16[16,72,2048]{2,1,0:T(8,128)(2,1)}), bf16[16,72,2048]{2,1,0:T(8,128)(2,1)}, u32[]{:S(2)}, u32[]{:S(2)}) async-start(bf16[16,72,2048]{2,1,0:T(8,128)(2,1)} %bitcast.49), calls=%async_computation.3 | async-start | bytes 9437184 | tf_op jit(solution)/shard_map/all_to_all | solution.py:75
  301.5 6.8 %gather_fusion.2 = bf16[1024]{0:T(1024)(128)(2,1)S(1)} fusion(bf16[1152]{0:T(1024)(128)(2,1)S(1)} %reshape.148, s32[1024]{0:T(1024)S(1)} %broadcast_clamp_fusion), kind=kCustom, calls=%fused_computation.4 | custom fusion | bytes 8192 | tf_op jit(solution)/shard_map/gather | solution.py:79
  308.4 0.7 copy.26
  309.1 96.0 %all-to-all-done.3 = bf16[16,72,2048]{2,1,0:T(8,128)(2,1)} async-done(((bf16[16,72,2048]{2,1,0:T(8,128)(2,1)}), bf16[16,72,2048]{2,1,0:T(8,128)(2,1)}, u32[]{:S(2)}, u32[]{:S(2)}) %all-to-all-start.3) | async-done | bytes 4718624 | tf_op jit(solution)/shard_map/all_to_all | solution.py:75
  405.0 11.8 %gather_fusion.1 = bf16[1024,2048]{1,0:T(8,128)(2,1)} fusion(bf16[1152,2048]{1,0:T(8,128)(2,1)} %bitcast.12, s32[1024]{0:T(1024)S(1)} %broadcast_clamp_fusion), kind=kCustom, calls=%fused_computation.3 | custom fusion | bytes 8392704 | tf_op jit(solution)/shard_map/gather | solution.py:78
  416.9 5.9 %bitcast_reduce_fusion = bf16[128,2048]{1,0:T(8,128)(2,1)} fusion(bf16[1024,2048]{1,0:T(8,128)(2,1)} %gather_fusion.1), kind=kLoop, calls=%fused_computation.10 | loop fusion | flops 1835008 | bytes 4718592 | tf_op jit(solution)/shard_map/reduce_sum | solution.py:81
  (40 shorter events, 2.1 us)
Async XLA Ops:
  7.2 26.7 %copy-start = (bf16[128,2048]{1,0:T(8,128)(2,1)S(1)}, bf16[128,2048]{1,0:T(8,128)(2,1)}, u32[]{:S(2)}) copy-start(bf16[128,2048]{1,0:T(8,128)(2,1)} %param.9) | copy-start | bytes 1572868
  27.4 26.9 %all-to-all-start = ((bf16[16,1,72]{2,1,0:T(2,128)(2,1)}), bf16[16,1,72]{2,1,0:T(2,128)(2,1)S(1)}, u32[]{:S(2)}, u32[]{:S(2)}) async-start(bf16[16,1,72]{2,1,0:T(2,128)(2,1)} %select_n.53), calls=%async_computation | async-start | bytes 16384 | tf_op jit(solution)/shard_map/all_to_all | solution.py:62
  33.9 5.9 %copy-start.1 = (bf16[128,2048]{1,0:T(8,128)(2,1)S(1)}, bf16[128,2048]{1,0:T(8,128)(2,1)}, u32[]{:S(2)}) copy-start(bf16[128,2048]{1,0:T(8,128)(2,1)} %param.10) | copy-start | bytes 1572868
  163.8 109.0 %all-to-all-start.1 = ((bf16[16,72,2048]{2,1,0:T(8,128)(2,1)}), bf16[16,72,2048]{2,1,0:T(8,128)(2,1)}, u32[]{:S(2)}, u32[]{:S(2)}) async-start(bf16[16,72,2048]{2,1,0:T(8,128)(2,1)} %bitcast.47), calls=%async_computation.1 | async-start | bytes 9437184 | tf_op jit(solution)/shard_map/all_to_all | solution.py:61
  169.1 30.0 %all-gather.11.cloned.1.call-start = ((), (), s32[]{:S(2)}) async-start(), calls=%async_computation.7 | async-start | bytes 2359296 | tf_op jit(solution)/shard_map/all_gather | solution.py:41
  169.8 58.1 %all-gather.9.cloned.1.call-start = ((), (), s32[]{:S(2)}) async-start(), calls=%async_computation.6 | async-start | bytes 2359296 | tf_op jit(solution)/shard_map/all_gather | solution.py:42
  170.6 86.1 %all-gather.7.cloned.1.call-start = ((), (), s32[]{:S(2)}) async-start(), calls=%async_computation.5 | async-start | bytes 2359296 | tf_op jit(solution)/shard_map/all_gather | solution.py:43
  280.3 15.0 %all-to-all-start.4 = ((bf16[16,1,72]{2,1,0:T(2,128)(2,1)}), bf16[16,1,72]{2,1,0:T(2,128)(2,1)S(1)}, u32[]{:S(2)}, u32[]{:S(2)}) async-start(bf16[16,1,72]{2,1,0:T(2,128)(2,1)} %convert_element_type.52), calls=%async_computation.4 | async-start | bytes 16384 | tf_op jit(solution)/shard_map/all_to_all | solution.py:76
  285.1 5.6 %copy-start.2 = (f32[1152,384]{0,1:T(8,128)S(1)}, f32[1152,384]{0,1:T(8,128)}, u32[]{:S(2)}) copy-start(f32[1152,384]{0,1:T(8,128)} %get-tuple-element.12) | copy-start | bytes 5308420
  285.1 5.6 %copy-start.3 = (bf16[1,2048,384]{2,1,0:T(8,128)(2,1)S(1)}, bf16[1,2048,384]{2,1,0:T(8,128)(2,1)}, u32[]{:S(2)}) copy-start(bf16[1,2048,384]{2,1,0:T(8,128)(2,1)} %all-gather.9.cloned.1.call-done) | copy-start | bytes 4718596
  295.3 109.7 %all-to-all-start.3 = ((bf16[16,72,2048]{2,1,0:T(8,128)(2,1)}), bf16[16,72,2048]{2,1,0:T(8,128)(2,1)}, u32[]{:S(2)}, u32[]{:S(2)}) async-start(bf16[16,72,2048]{2,1,0:T(8,128)(2,1)} %bitcast.49), calls=%async_computation.3 | async-start | bytes 9437184 | tf_op jit(solution)/shard_map/all_to_all | solution.py:75
Sparse Core Ops, SparseCore 0:
  171.4 27.6 all-gather.10
  200.7 27.1 all-gather.8
  229.4 27.1 all-gather.6
where the time goes:
time: 430 us; the launch traced here: 429 us
  waiting for transfers between devices  188 us (44%)
  blocking collectives  110 us (26%)
  local copies, waits for them, and re-layouts  46.7 us (11%)
  matrix products  28.4 us (7%)
  starting transfers between devices  22.9 us (5%)
  other arithmetic  19.9 us (5%)
  between operations  13.9 us (3%)
    all_to_all x1, blocking collectives, per_device(): lax.all_to_all(send_x, 'expert', split_axis=0, concat_axis=0, tiled=True)  110 us
    all_to_all x1, waiting for transfers between devices, per_device(): lax.all_to_all(out_grad, 'expert', split_axis=0, concat_axis=0, tiled=True)  96 us
    all_gather x1, waiting for transfers between devices, per_device(): lax.all_gather(w_gate[0], 'dp', axis=0, tiled=True)  27.7 us
    all_gather x1, waiting for transfers between devices, per_device(): lax.all_gather(w_up[0], 'dp', axis=0, tiled=True)  23.7 us
    all_gather x1, waiting for transfers between devices, per_device(): lax.all_gather(w_down[0], 'dp', axis=1, tiled=True)  22.5 us
    all_to_all x1, waiting for transfers between devices, per_device(): lax.all_to_all(send_g, 'expert', split_axis=0, concat_axis=0, tiled=True)  16.1 us
    gather x1, local copies, waits for them, and re-layouts, per_device(): part_flat = back_grad.reshape(slots_all, width_model)[placed]  11.8 us
  transfers between devices with their start and end apart: 7, of which 5 were waited for; matrix products, arithmetic and copies ran while one was open for 12% of the time, Pallas kernels for 0%

commit v1 on v0

--- a/solution.py
+++ b/solution.py
@@ -2,6 +2,31 @@
 import jax.numpy as jnp
 from jax import lax
 from jax.sharding import PartitionSpec as P
+
+
+def _resolve_plane(inp, array_dim, vals):
+    top, prior = (inp.shape[:array_dim], inp.shape[array_dim + 1 :])
+    return jnp.moveaxis(inp.reshape(*top, vals, -1, *prior), array_dim, 0)
+
+
+def open_ranges_now(z, in_dim):
+    local_next = list(z.shape[1:])
+    local_next[in_dim] *= z.shape[0]
+    return jnp.moveaxis(z, 0, in_dim).reshape(local_next)
+
+
+def meet_circles(u_in, link_axis, v0, here_x):
+    reached = lax.psum(1, link_axis)
+    r2 = lax.axis_index(link_axis)
+    shaped, b_now = (reached, r2)
+    x_new = _resolve_plane(u_in, v0, shaped)
+    history = [x_new[b_now]]
+    for dev_i in tuple(range(1, shaped)):
+        step_out = x_new[b_now ^ dev_i]
+        history.append(lax.ppermute(step_out, link_axis, [(d, d ^ dev_i) for d in range(shaped)]))
+    current_arr = jnp.stack(history)
+    x_new = current_arr[b_now ^ jnp.arange(shaped)]
+    return open_ranges_now(x_new, here_x)
 
 
 def expert_rows(x_rows, g_rows, weight_rows, gate_mat, up_mat, down_mat):
@@ -72,7 +97,7 @@
     out_grad = out_grad.reshape(n_expert, capacity, width_model)
     out_route = out_route.reshape(n_expert, capacity)
     back_grad, back_route = (
-        lax.all_to_all(out_grad, "expert", split_axis=0, concat_axis=0, tiled=True),
+        meet_circles(out_grad, "expert", 0, 0),
         lax.all_to_all(out_route, "expert", split_axis=0, concat_axis=0, tiled=True),
     )
     part_flat = back_grad.reshape(slots_all, width_model)[placed]

time: 430 us -> 448 us (1.042)
  local copies, waits for them, and re-layouts: 46.7 us -> 69.6 us
  waiting for transfers between devices: 188 us -> 170 us
  starting transfers between devices: 22.9 us -> 39.8 us
    all_to_all x1 -> x0, waiting for transfers between devices: 96 us -> none  [per_device(): lax.all_to_all(out_grad, 'expert', split_axis=0, concat_axis=0, tiled=True)]
    ppermute x0 -> x15, waiting for transfers between devices: none -> 78.1 us  [meet_circles(): lax.ppermute(step_out, link_axis, [(d, d ^ dev_i) for d in range(shaped)])]
    ppermute x0 -> x15, starting transfers between devices: none -> 22.7 us  [meet_circles(): lax.ppermute(step_out, link_axis, [(d, d ^ dev_i) for d in range(shaped)])]
    unnamed x11 -> x27, local copies, waits for them, and re-layouts: 2.27 us -> 17.4 us
    all_to_all x1 -> x0, starting transfers between devices: 6.03 us -> none  [per_device(): lax.all_to_all(out_grad, 'expert', split_axis=0, concat_axis=0, tiled=True)]
    gather x0 -> x1, local copies, waits for them, and re-layouts: none -> 5.35 us  [meet_circles(): x_new = current_arr[b_now ^ jnp.arange(shaped)]]
  transfers between devices with their start and end apart: 7 -> 21, of which waited for: 5 -> 14; matrix products, arithmetic and copies ran while one was open for 12% -> 12% of each run, Pallas kernels for 0% -> 0%
where the time goes in v1:
time: 448 us; the launch traced here: 447 us
  waiting for transfers between devices  170 us (38%)
  blocking collectives  110 us (25%)
  local copies, waits for them, and re-layouts  69.6 us (16%)
  starting transfers between devices  39.8 us (9%)
  matrix products  24.4 us (5%)
  other arithmetic  19.9 us (4%)
  between operations  14 us (3%)
    all_to_all x1, blocking collectives, per_device(): lax.all_to_all(send_x, 'expert', split_axis=0, concat_axis=0, tiled=True)  110 us
    ppermute x15, waiting for transfers between devices, meet_circles(): lax.ppermute(step_out, link_axis, [(d, d ^ dev_i) for d in range(shaped)])  78.1 us
    all_gather x1, waiting for transfers between devices, per_device(): lax.all_gather(w_gate[0], 'dp', axis=0, tiled=True)  27.6 us
    all_gather x1, waiting for transfers between devices, per_device(): lax.all_gather(w_up[0], 'dp', axis=0, tiled=True)  23.7 us
    ppermute x15, starting transfers between devices, meet_circles(): lax.ppermute(step_out, link_axis, [(d, d ^ dev_i) for d in range(shaped)])  22.7 us
    all_gather x1, waiting for transfers between devices, per_device(): lax.all_gather(w_down[0], 'dp', axis=1, tiled=True)  22.4 us
    unnamed x27, local copies, waits for them, and re-layouts  17.4 us
    all_to_all x1, waiting for transfers between devices, per_device(): lax.all_to_all(send_g, 'expert', split_axis=0, concat_axis=0, tiled=True)  16.1 us
  transfers between devices with their start and end apart: 21, of which 14 were waited for; matrix products, arithmetic and copies ran while one was open for 12% of the time, Pallas kernels for 0%

profile of v1, /device:TPU:11, one launch (start us, length us, event | category | flops | bytes accessed | tf_op | source)
XLA Modules:
  0.0 447.4 jit_solution(5916201725483968552)
XLA Ops:
  8.9 4.5 %reduce-window.6 = s32[16,8,128]{2,1,0:T(8,128)S(1)} reduce-window(s32[16,8,128]{2,1,0:T(8,128)S(1)} %fusion.18, s32[]{:T(128)} %constant.36.clone.1), window={size=1x1x128 pad=0_0x0_0x127_0}, to_apply=%region_0.0 | reduce-window | flops 2080768 | bytes 131076 | tf_op jit(solution)/shard_map/reduce-window
  14.1 4.3 scatter_custom_fusion
  19.4 7.3 %gather_fusion = bf16[1152]{0:T(1024)(128)(2,1)S(1)} fusion(bf16[1024]{0:T(1024)(128)(2,1)S(1)} %reshape.150, s32[2048]{0:T(1024)S(1)} %get-tuple-element.30), kind=kCustom, calls=%fused_computation.2 | custom fusion | bytes 9216 | tf_op jit(solution)/shard_map/jit(_take)/gather | solution.py:54
  27.4 6.5 %all-to-all-start = ((bf16[16,1,72]{2,1,0:T(2,128)(2,1)}), bf16[16,1,72]{2,1,0:T(2,128)(2,1)S(1)}, u32[]{:S(2)}, u32[]{:S(2)}) async-start(bf16[16,1,72]{2,1,0:T(2,128)(2,1)} %select_n.128), calls=%async_computation | async-start | bytes 16384 | tf_op jit(solution)/shard_map/all_to_all | solution.py:87
  33.9 5.9 %gather_fusion.4 = bf16[1152,2048]{1,0:T(8,128)(2,1)} fusion(bf16[128,2048]{1,0:T(8,128)(2,1)S(1)} %copy-done, s32[2048]{0:T(1024)S(1)} %get-tuple-element.29), kind=kCustom, calls=%fused_computation.clone | custom fusion | bytes 9441792 | tf_op jit(solution)/shard_map/jit(_take)/gather | solution.py:53
  39.8 6.0 %gather_fusion.5 = bf16[1152,2048]{1,0:T(8,128)(2,1)} fusion(bf16[128,2048]{1,0:T(8,128)(2,1)S(1)} %copy-done.2, s32[2048]{0:T(1024)S(1)} %get-tuple-element.29), kind=kCustom, calls=%fused_computation.1.clone | custom fusion | bytes 9441792 | tf_op jit(solution)/shard_map/jit(_take)/gather | solution.py:52
  45.8 8.5 %broadcast_select_fusion.1 = (bf16[1152,2048]{1,0:T(8,128)(2,1)}, bf16[1152,2048]{1,0:T(8,128)(2,1)}) fusion(bf16[1152,2048]{1,0:T(8,128)(2,1)} %gather_fusion.4, pred[1152]{0:T(1024)(128)(4,1)S(1)} %get-tuple-element.7, bf16[1152,2048]{1,0:T(8,128)(2,1)} %gather_fusion.5), kind=kLoop, calls=%fused_computation.10 | loop fusion | flops 4718592 | bytes 18875520 | tf_op jit(solution)/shard_map/jit(_take)/select_n | solution.py:53
  54.3 109.6 %all_to_all.22 = bf16[16,72,2048]{2,1,0:T(8,128)(2,1)} all-to-all(bf16[16,72,2048]{2,1,0:T(8,128)(2,1)} %bitcast.111), channel_id=1, replica_groups=mesh['dp'=2,'expert'=16] {'expert'}, dimensions={0} | all-to-all | bytes 9437184 | tf_op jit(solution)/shard_map/all_to_all | solution.py:85
  163.9 5.3 %all-to-all-start.1 = ((bf16[16,72,2048]{2,1,0:T(8,128)(2,1)}), bf16[16,72,2048]{2,1,0:T(8,128)(2,1)}, u32[]{:S(2)}, u32[]{:S(2)}) async-start(bf16[16,72,2048]{2,1,0:T(8,128)(2,1)} %bitcast.110), calls=%async_computation.1 | async-start | bytes 9437184 | tf_op jit(solution)/shard_map/all_to_all | solution.py:86
  171.6 27.6 %all-gather.11.cloned.1.call-done = bf16[1,2048,384]{2,1,0:T(8,128)(2,1)} async-done(((bf16[1,1024,384]{2,1,0:T(8,128)(2,1)}), bf16[1,2048,384]{2,1,0:T(8,128)(2,1)}) %all-gather.11.cloned.1.call-update) | async-done | bytes 1572880 | tf_op jit(solution)/shard_map/all_gather | solution.py:66
  199.2 5.1 %fusion.4 = f32[1152,384]{0,1:T(8,128)S(1)} fusion(bf16[1152,2048]{1,0:T(8,128)(2,1)} %bitcast.114, bf16[1,2048,384]{2,1,0:T(8,128)(2,1)} %all-gather.11.cloned.1.call-done), kind=kOutput, calls=%fused_computation.19 | convolution fusion | flops 1811939328 | bytes 8060928 | tf_op jit(solution)/shard_map/dot_general | solution.py:33
  204.3 23.7 %all-gather.9.cloned.1.call-done = bf16[1,2048,384]{2,1,0:T(8,128)(2,1)} async-done(((bf16[1,1024,384]{2,1,0:T(8,128)(2,1)}), bf16[1,2048,384]{2,1,0:T(8,128)(2,1)}) %all-gather.9.cloned.1.call-update) | async-done | bytes 1572880 | tf_op jit(solution)/shard_map/all_gather | solution.py:67
  228.0 6.3 %fusion.7 = f32[1152,384]{0,1:T(8,128)} fusion(bf16[1152,2048]{1,0:T(8,128)(2,1)} %bitcast.115, bf16[1,2048,384]{2,1,0:T(8,128)(2,1)} %all-gather.9.cloned.1.call-done), kind=kOutput, calls=%fused_computation.22 | convolution fusion | flops 1811939328 | bytes 8060928 | tf_op jit(solution)/shard_map/dot_general | solution.py:34
  234.3 22.4 %all-gather.7.cloned.1.call-done = bf16[1,384,2048]{2,1,0:T(8,128)(2,1)} async-done(((bf16[1,384,1024]{2,1,0:T(8,128)(2,1)}), bf16[1,384,2048]{2,1,0:T(8,128)(2,1)}) %all-gather.7.cloned.1.call-update) | async-done | bytes 1572880 | tf_op jit(solution)/shard_map/all_gather | solution.py:68
  256.7 16.1 %all-to-all-done.1 = bf16[16,72,2048]{2,1,0:T(8,128)(2,1)} async-done(((bf16[16,72,2048]{2,1,0:T(8,128)(2,1)}), bf16[16,72,2048]{2,1,0:T(8,128)(2,1)}, u32[]{:S(2)}, u32[]{:S(2)}) %all-to-all-start.1) | async-done | bytes 4718624 | tf_op jit(solution)/shard_map/all_to_all | solution.py:86
  272.9 5.8 %multiply_reduce_fusion = (bf16[1152]{0:T(1024)(128)(2,1)S(1)}, f32[1152,384]{0,1:T(8,128)S(1)}) fusion(f32[1152,384]{0,1:T(8,128)} %fusion.7, f32[1152,384]{0,1:T(8,128)S(1)} %fusion.4, bf16[1152,2048]{1,0:T(8,128)(2,1)} %bitcast.5, bf16[1,384,2048]{2,1,0:T(8,128)(2,1)} %all-gather.7.cloned.1.call-done), kind=kOutput, calls=%fused_computation.12 | convolution fusion | flops 1815034752 | bytes 11602176 | tf_op jit(solution)/shard_map/dot_general | solution.py:38
  278.7 3.0 fusion.2
  281.7 4.2 fusion
  288.3 5.0 %all-to-all-start.3 = ((bf16[16,1,72]{2,1,0:T(2,128)(2,1)}), bf16[16,1,72]{2,1,0:T(2,128)(2,1)S(1)}, u32[]{:S(2)}, u32[]{:S(2)}) async-start(bf16[16,1,72]{2,1,0:T(2,128)(2,1)} %convert_element_type.52), calls=%async_computation.3 | async-start | bytes 16384 | tf_op jit(solution)/shard_map/all_to_all | solution.py:101
  297.4 6.8 %gather_fusion.3 = bf16[1024]{0:T(1024)(128)(2,1)S(1)} fusion(bf16[1152]{0:T(1024)(128)(2,1)S(1)} %reshape.156, s32[1024]{0:T(1024)S(1)} %broadcast_clamp_fusion), kind=kCustom, calls=%fused_computation.5 | custom fusion | bytes 8192 | tf_op jit(solution)/shard_map/gather | solution.py:104
  320.5 4.3 collective-permute-done.5
  324.8 5.2 %collective-permute-start.10 = (bf16[1,72,2048]{2,1,0:T(8,128)(2,1)S(1)}, bf16[1,72,2048]{2,1,0:T(8,128)(2,1)S(1)}, u32[]{:S(2)}, u32[]{:S(2)}) collective-permute-start(bf16[1,72,2048]{2,1,0:T(8,128)(2,1)S(1)} %get-tuple-element.13), channel_id=1, source_target_pairs={{0,11},{1,10},{2,9},{3,8},{4,15},{5,14},{6,13},{7,12},{8,3},{9,2},... | collective-permute-start | bytes 884744 | tf_op jit(solution)/shard_map/ppermute | solution.py:26
  334.9 28.9 %collective-permute-done.8 = bf16[1,72,2048]{2,1,0:T(8,128)(2,1)S(1)} collective-permute-done((bf16[1,72,2048]{2,1,0:T(8,128)(2,1)S(1)}, bf16[1,72,2048]{2,1,0:T(8,128)(2,1)S(1)}, u32[]{:S(2)}, u32[]{:S(2)}) %collective-permute-start.8) | collective-permute-done | bytes 294944 | tf_op jit(solution)/shard_map/ppermute | solution.py:26
  366.7 9.8 %collective-permute-done.9 = bf16[1,72,2048]{2,1,0:T(8,128)(2,1)S(1)} collective-permute-done((bf16[1,72,2048]{2,1,0:T(8,128)(2,1)S(1)}, bf16[1,72,2048]{2,1,0:T(8,128)(2,1)S(1)}, u32[]{:S(2)}, u32[]{:S(2)}) %collective-permute-start.9) | collective-permute-done | bytes 294944 | tf_op jit(solution)/shard_map/ppermute | solution.py:26
  379.4 3.3 collective-permute-done.10
  383.4 13.6 %collective-permute-done.11 = bf16[1,72,2048]{2,1,0:T(8,128)(2,1)S(1)} collective-permute-done((bf16[1,72,2048]{2,1,0:T(8,128)(2,1)S(1)}, bf16[1,72,2048]{2,1,0:T(8,128)(2,1)S(1)}, u32[]{:S(2)}, u32[]{:S(2)}) %collective-permute-start.11) | collective-permute-done | bytes 294944 | tf_op jit(solution)/shard_map/ppermute | solution.py:26
  397.7 5.6 %collective-permute-done.12 = bf16[1,72,2048]{2,1,0:T(8,128)(2,1)S(1)} collective-permute-done((bf16[1,72,2048]{2,1,0:T(8,128)(2,1)S(1)}, bf16[1,72,2048]{2,1,0:T(8,128)(2,1)S(1)}, u32[]{:S(2)}, u32[]{:S(2)}) %collective-permute-start.12) | collective-permute-done | bytes 294944 | tf_op jit(solution)/shard_map/ppermute | solution.py:26
  404.1 6.7 %collective-permute-done.13 = bf16[1,72,2048]{2,1,0:T(8,128)(2,1)S(1)} collective-permute-done((bf16[1,72,2048]{2,1,0:T(8,128)(2,1)S(1)}, bf16[1,72,2048]{2,1,0:T(8,128)(2,1)S(1)}, u32[]{:S(2)}, u32[]{:S(2)}) %collective-permute-start.13) | collective-permute-done | bytes 294944 | tf_op jit(solution)/shard_map/ppermute | solution.py:26
  411.5 5.6 %collective-permute-done.14 = bf16[1,72,2048]{2,1,0:T(8,128)(2,1)S(1)} collective-permute-done((bf16[1,72,2048]{2,1,0:T(8,128)(2,1)S(1)}, bf16[1,72,2048]{2,1,0:T(8,128)(2,1)S(1)}, u32[]{:S(2)}, u32[]{:S(2)}) %collective-permute-start.14) | collective-permute-done | bytes 294944 | tf_op jit(solution)/shard_map/ppermute | solution.py:26
  417.8 5.4 %gather_fusion.1 = bf16[16,72,2048]{2,1,0:T(8,128)(2,1)} fusion(bf16[16,72,2048]{2,1,0:T(8,128)(2,1)} %bitcast.113, s32[1024]{0:T(1024)S(1)} %pad_clamp_fusion.2), kind=kCustom, calls=%fused_computation.3 | custom fusion | bytes 9437248 | tf_op jit(solution)/shard_map/gather | solution.py:28
  423.2 11.8 %gather_fusion.2 = bf16[1024,2048]{1,0:T(8,128)(2,1)} fusion(bf16[1152,2048]{1,0:T(8,128)(2,1)} %bitcast.109, s32[1024]{0:T(1024)S(1)} %broadcast_clamp_fusion), kind=kCustom, calls=%fused_computation.4 | custom fusion | bytes 8392704 | tf_op jit(solution)/shard_map/gather | solution.py:103
  435.0 5.9 %bitcast_reduce_fusion = bf16[128,2048]{1,0:T(8,128)(2,1)} fusion(bf16[1024,2048]{1,0:T(8,128)(2,1)} %gather_fusion.2), kind=kLoop, calls=%fused_computation.11 | loop fusion | flops 1835008 | bytes 4718592 | tf_op jit(solution)/shard_map/reduce_sum | solution.py:106
  (88 shorter events, 43.4 us)
Async XLA Ops:
  7.2 26.7 %copy-start = (bf16[128,2048]{1,0:T(8,128)(2,1)S(1)}, bf16[128,2048]{1,0:T(8,128)(2,1)}, u32[]{:S(2)}) copy-start(bf16[128,2048]{1,0:T(8,128)(2,1)} %param.10) | copy-start | bytes 1572868
  27.4 27.0 %all-to-all-start = ((bf16[16,1,72]{2,1,0:T(2,128)(2,1)}), bf16[16,1,72]{2,1,0:T(2,128)(2,1)S(1)}, u32[]{:S(2)}, u32[]{:S(2)}) async-start(bf16[16,1,72]{2,1,0:T(2,128)(2,1)} %select_n.128), calls=%async_computation | async-start | bytes 16384 | tf_op jit(solution)/shard_map/all_to_all | solution.py:87
  33.9 5.9 %copy-start.2 = (bf16[128,2048]{1,0:T(8,128)(2,1)S(1)}, bf16[128,2048]{1,0:T(8,128)(2,1)}, u32[]{:S(2)}) copy-start(bf16[128,2048]{1,0:T(8,128)(2,1)} %param.9) | copy-start | bytes 1572868
  163.9 109.0 %all-to-all-start.1 = ((bf16[16,72,2048]{2,1,0:T(8,128)(2,1)}), bf16[16,72,2048]{2,1,0:T(8,128)(2,1)}, u32[]{:S(2)}, u32[]{:S(2)}) async-start(bf16[16,72,2048]{2,1,0:T(8,128)(2,1)} %bitcast.110), calls=%async_computation.1 | async-start | bytes 9437184 | tf_op jit(solution)/shard_map/all_to_all | solution.py:86
  169.2 30.0 %all-gather.11.cloned.1.call-start = ((), (), s32[]{:S(2)}) async-start(), calls=%async_computation.6 | async-start | bytes 2359296 | tf_op jit(solution)/shard_map/all_gather | solution.py:66
  169.9 58.1 %all-gather.9.cloned.1.call-start = ((), (), s32[]{:S(2)}) async-start(), calls=%async_computation.5 | async-start | bytes 2359296 | tf_op jit(solution)/shard_map/all_gather | solution.py:67
  170.6 86.1 %all-gather.7.cloned.1.call-start = ((), (), s32[]{:S(2)}) async-start(), calls=%async_computation.4 | async-start | bytes 2359296 | tf_op jit(solution)/shard_map/all_gather | solution.py:68
  272.9 5.8 %copy-start.3 = (f32[1152,384]{0,1:T(8,128)S(1)}, f32[1152,384]{0,1:T(8,128)}, u32[]{:S(2)}) copy-start(f32[1152,384]{0,1:T(8,128)} %fusion.7) | copy-start | bytes 5308420
  272.9 5.8 %copy-start.4 = (bf16[1,2048,384]{2,1,0:T(8,128)(2,1)S(1)}, bf16[1,2048,384]{2,1,0:T(8,128)(2,1)}, u32[]{:S(2)}) copy-start(bf16[1,2048,384]{2,1,0:T(8,128)(2,1)} %all-gather.11.cloned.1.call-done) | copy-start | bytes 4718596
  287.5 17.4 %collective-permute-start = (bf16[1,72,2048]{2,1,0:T(8,128)(2,1)}, bf16[1,72,2048]{2,1,0:T(8,128)(2,1)}, u32[]{:S(2)}, u32[]{:S(2)}) collective-permute-start(bf16[1,72,2048]{2,1,0:T(8,128)(2,1)} %get-tuple-element.23), channel_id=1, source_target_pairs={{0,1},{1,0},{2,3},{3,2},{4,5},{5,4},{6,7},{7,6},{8,9},{9,8},{10,11... | collective-permute-start | bytes 884744 | tf_op jit(solution)/shard_map/ppermute | solution.py:26
  288.3 8.9 %all-to-all-start.3 = ((bf16[16,1,72]{2,1,0:T(2,128)(2,1)}), bf16[16,1,72]{2,1,0:T(2,128)(2,1)S(1)}, u32[]{:S(2)}, u32[]{:S(2)}) async-start(bf16[16,1,72]{2,1,0:T(2,128)(2,1)} %convert_element_type.52), calls=%async_computation.3 | async-start | bytes 16384 | tf_op jit(solution)/shard_map/all_to_all | solution.py:101
  293.4 15.3 %collective-permute-start.1 = (bf16[1,72,2048]{2,1,0:T(8,128)(2,1)}, bf16[1,72,2048]{2,1,0:T(8,128)(2,1)}, u32[]{:S(2)}, u32[]{:S(2)}) collective-permute-start(bf16[1,72,2048]{2,1,0:T(8,128)(2,1)} %get-tuple-element.22), channel_id=1, source_target_pairs={{0,2},{1,3},{2,0},{3,1},{4,6},{5,7},{6,4},{7,5},{8,10},{9,11},{10,... | collective-permute-start | bytes 884744 | tf_op jit(solution)/shard_map/ppermute | solution.py:26
  293.7 17.8 %collective-permute-start.2 = (bf16[1,72,2048]{2,1,0:T(8,128)(2,1)}, bf16[1,72,2048]{2,1,0:T(8,128)(2,1)}, u32[]{:S(2)}, u32[]{:S(2)}) collective-permute-start(bf16[1,72,2048]{2,1,0:T(8,128)(2,1)} %get-tuple-element.21), channel_id=1, source_target_pairs={{0,3},{1,2},{2,1},{3,0},{4,7},{5,6},{6,5},{7,4},{8,11},{9,10},{10,... | collective-permute-start | bytes 884744 | tf_op jit(solution)/shard_map/ppermute | solution.py:26
  295.5 19.3 %collective-permute-start.3 = (bf16[1,72,2048]{2,1,0:T(8,128)(2,1)}, bf16[1,72,2048]{2,1,0:T(8,128)(2,1)}, u32[]{:S(2)}, u32[]{:S(2)}) collective-permute-start(bf16[1,72,2048]{2,1,0:T(8,128)(2,1)} %get-tuple-element.20), channel_id=1, source_target_pairs={{0,4},{1,5},{2,6},{3,7},{4,0},{5,1},{6,2},{7,3},{8,12},{9,13},{10,... | collective-permute-start | bytes 884744 | tf_op jit(solution)/shard_map/ppermute | solution.py:26
  295.8 21.6 %collective-permute-start.4 = (bf16[1,72,2048]{2,1,0:T(8,128)(2,1)S(1)}, bf16[1,72,2048]{2,1,0:T(8,128)(2,1)}, u32[]{:S(2)}, u32[]{:S(2)}) collective-permute-start(bf16[1,72,2048]{2,1,0:T(8,128)(2,1)S(1)} %get-tuple-element.19), channel_id=1, source_target_pairs={{0,5},{1,4},{2,7},{3,6},{4,1},{5,0},{6,3},{7,2},{8,13},{9,12},{10,... | collective-permute-start | bytes 884744 | tf_op jit(solution)/shard_map/ppermute | solution.py:26
  304.9 19.9 %collective-permute-start.5 = (bf16[1,72,2048]{2,1,0:T(8,128)(2,1)S(1)}, bf16[1,72,2048]{2,1,0:T(8,128)(2,1)S(1)}, u32[]{:S(2)}, u32[]{:S(2)}) collective-permute-start(bf16[1,72,2048]{2,1,0:T(8,128)(2,1)S(1)} %get-tuple-element.18), channel_id=1, source_target_pairs={{0,6},{1,7},{2,4},{3,5},{4,2},{5,3},{6,0},{7,1},{8,14},{9,15},{10,... | collective-permute-start | bytes 884744 | tf_op jit(solution)/shard_map/ppermute | solution.py:26
  308.7 22.5 %collective-permute-start.6 = (bf16[1,72,2048]{2,1,0:T(8,128)(2,1)S(1)}, bf16[1,72,2048]{2,1,0:T(8,128)(2,1)S(1)}, u32[]{:S(2)}, u32[]{:S(2)}) collective-permute-start(bf16[1,72,2048]{2,1,0:T(8,128)(2,1)S(1)} %get-tuple-element.17), channel_id=1, source_target_pairs={{0,7},{1,6},{2,5},{3,4},{4,3},{5,2},{6,1},{7,0},{8,15},{9,14},{10,... | collective-permute-start | bytes 884744 | tf_op jit(solution)/shard_map/ppermute | solution.py:26
  311.5 22.0 %collective-permute-start.7 = (bf16[1,72,2048]{2,1,0:T(8,128)(2,1)S(1)}, bf16[1,72,2048]{2,1,0:T(8,128)(2,1)S(1)}, u32[]{:S(2)}, u32[]{:S(2)}) collective-permute-start(bf16[1,72,2048]{2,1,0:T(8,128)(2,1)S(1)} %get-tuple-element.16), channel_id=1, source_target_pairs={{0,8},{1,9},{2,10},{3,11},{4,12},{5,13},{6,14},{7,15},{8,0},{9,1},... | collective-permute-start | bytes 884744 | tf_op jit(solution)/shard_map/ppermute | solution.py:26
  314.7 49.1 %collective-permute-start.8 = (bf16[1,72,2048]{2,1,0:T(8,128)(2,1)S(1)}, bf16[1,72,2048]{2,1,0:T(8,128)(2,1)S(1)}, u32[]{:S(2)}, u32[]{:S(2)}) collective-permute-start(bf16[1,72,2048]{2,1,0:T(8,128)(2,1)S(1)} %get-tuple-element.15), channel_id=1, source_target_pairs={{0,9},{1,8},{2,11},{3,10},{4,13},{5,12},{6,15},{7,14},{8,1},{9,0},... | collective-permute-start | bytes 884744 | tf_op jit(solution)/shard_map/ppermute | solution.py:26
  317.4 59.1 %collective-permute-start.9 = (bf16[1,72,2048]{2,1,0:T(8,128)(2,1)S(1)}, bf16[1,72,2048]{2,1,0:T(8,128)(2,1)S(1)}, u32[]{:S(2)}, u32[]{:S(2)}) collective-permute-start(bf16[1,72,2048]{2,1,0:T(8,128)(2,1)S(1)} %get-tuple-element.14), channel_id=1, source_target_pairs={{0,10},{1,11},{2,8},{3,9},{4,14},{5,15},{6,12},{7,13},{8,2},{9,3},... | collective-permute-start | bytes 884744 | tf_op jit(solution)/shard_map/ppermute | solution.py:26
  324.8 57.8 %collective-permute-start.10 = (bf16[1,72,2048]{2,1,0:T(8,128)(2,1)S(1)}, bf16[1,72,2048]{2,1,0:T(8,128)(2,1)S(1)}, u32[]{:S(2)}, u32[]{:S(2)}) collective-permute-start(bf16[1,72,2048]{2,1,0:T(8,128)(2,1)S(1)} %get-tuple-element.13), channel_id=1, source_target_pairs={{0,11},{1,10},{2,9},{3,8},{4,15},{5,14},{6,13},{7,12},{8,3},{9,2},... | collective-permute-start | bytes 884744 | tf_op jit(solution)/shard_map/ppermute | solution.py:26
  331.2 65.8 %collective-permute-start.11 = (bf16[1,72,2048]{2,1,0:T(8,128)(2,1)S(1)}, bf16[1,72,2048]{2,1,0:T(8,128)(2,1)S(1)}, u32[]{:S(2)}, u32[]{:S(2)}) collective-permute-start(bf16[1,72,2048]{2,1,0:T(8,128)(2,1)S(1)} %get-tuple-element.12), channel_id=1, source_target_pairs={{0,12},{1,13},{2,14},{3,15},{4,8},{5,9},{6,10},{7,11},{8,4},{9,5},... | collective-permute-start | bytes 884744 | tf_op jit(solution)/shard_map/ppermute | solution.py:26
  333.5 69.9 %collective-permute-start.12 = (bf16[1,72,2048]{2,1,0:T(8,128)(2,1)S(1)}, bf16[1,72,2048]{2,1,0:T(8,128)(2,1)S(1)}, u32[]{:S(2)}, u32[]{:S(2)}) collective-permute-start(bf16[1,72,2048]{2,1,0:T(8,128)(2,1)S(1)} %get-tuple-element.11), channel_id=1, source_target_pairs={{0,13},{1,12},{2,15},{3,14},{4,9},{5,8},{6,11},{7,10},{8,5},{9,4},... | collective-permute-start | bytes 884744 | tf_op jit(solution)/shard_map/ppermute | solution.py:26
  363.9 46.9 %collective-permute-start.13 = (bf16[1,72,2048]{2,1,0:T(8,128)(2,1)S(1)}, bf16[1,72,2048]{2,1,0:T(8,128)(2,1)S(1)}, u32[]{:S(2)}, u32[]{:S(2)}) collective-permute-start(bf16[1,72,2048]{2,1,0:T(8,128)(2,1)S(1)} %get-tuple-element.10), channel_id=1, source_target_pairs={{0,14},{1,15},{2,12},{3,13},{4,10},{5,11},{6,8},{7,9},{8,6},{9,7},... | collective-permute-start | bytes 884744 | tf_op jit(solution)/shard_map/ppermute | solution.py:26
  376.5 40.6 %collective-permute-start.14 = (bf16[1,72,2048]{2,1,0:T(8,128)(2,1)S(1)}, bf16[1,72,2048]{2,1,0:T(8,128)(2,1)S(1)}, u32[]{:S(2)}, u32[]{:S(2)}) collective-permute-start(bf16[1,72,2048]{2,1,0:T(8,128)(2,1)S(1)} %get-tuple-element.9), channel_id=1, source_target_pairs={{0,15},{1,14},{2,13},{3,12},{4,11},{5,10},{6,9},{7,8},{8,7},{9,6},... | collective-permute-start | bytes 884744 | tf_op jit(solution)/shard_map/ppermute | solution.py:26
  423.2 17.7 %copy-start.1 = (bf16[128,2048]{1,0:T(8,128)(2,1)S(1)}, bf16[128,2048]{1,0:T(8,128)(2,1)}, u32[]{:S(2)}) copy-start(bf16[128,2048]{1,0:T(8,128)(2,1)} %param.10) | copy-start | bytes 1572868
Sparse Core Ops, SparseCore 0:
  171.5 27.6 all-gather.10
  200.7 27.1 all-gather.8
  229.5 27.1 all-gather.6
